TPU v7x, 32 devices: a whole 2x2x4 slice. The times are simulated.
32 devices in a mesh: seq: 16 (over z, x, core), head: 2 (over y).
Axes of the slice: x: 2, y: 2, z: 4, core: 2. Of those that a mesh axis runs over, the one named last changes fastest.
Arguments:
- queries: bfloat16 [16384, 2048], P(('seq', 'head')), may hold values from -6 to 6
- key_rows: bfloat16 [16384, 2048], P(('seq', 'head')), may hold values from -6 to 6
- values: bfloat16 [16384, 4096], P(('seq', 'head')), may hold values from -140 to 140
- in_gate: bfloat16 [16384, 8], P(('seq', 'head')), may hold values from -6 to 226
- forget_gate: bfloat16 [16384, 8], P(('seq', 'head')), may hold values from -0.25 to 15
- out_gate: bfloat16 [16384, 4096], P(('seq', 'head')), may hold values from -6 to 6
- norm_gain: float32 [4096], P('head'), may hold values from 0.1 to 1.9
Outputs:
- layer_out: bfloat16 [16384, 4096], P(('seq', 'head'))
All inputs are finite; a program needn't handle non-finite values.
Results may differ from a plain program's by a relative error of at most 0.0085.
Values may be sent and summed in bfloat16 or wider, within the bound.
A program may use at most 192 MiB of HBM per device.

v0:
```python
import jax
import jax.numpy as jnp
from jax import lax
from jax.sharding import PartitionSpec as P

STRETCH = 1024


far_below = -1e30
norm_eps = 1e-06


def prefix_2(part, axis, combine, identity):
    place = lax.axis_index(axis)
    gathered = jax.tree.map(lambda a: lax.all_gather(a, axis), part)
    state = jax.tree.map(lambda a, e: jnp.zeros_like(a) + jnp.asarray(e, a.dtype), part, identity)

    def one(step, state):
        return combine(
            state, jax.tree.map(lambda a: lax.dynamic_index_in_dim(a, step, 0, False), gathered)
        )

    return lax.fori_loop(0, place, one, state)


def combine(earlier, later):
    state_a, max_a, decay_a = earlier
    state_b, max_b, decay_b = later
    shifted = max_a + decay_b
    joint_max = jnp.maximum(shifted, max_b)
    state_total_sum = (
        jnp.exp(shifted - joint_max)[..., None, None] * state_a
        + jnp.exp(max_b - joint_max)[..., None, None] * state_b
    )
    return (state_total_sum, joint_max, decay_a + decay_b)


def summarize(keys_blk, values_block, in_blk, forget_blk):
    log_forget = jax.nn.log_sigmoid(forget_blk.astype(jnp.float32))
    running = jnp.cumsum(log_forget, axis=0)
    final_cum = running[-1]
    log_weight = final_cum[None, :] - running + in_blk.astype(jnp.float32)
    block_max = jnp.max(log_weight, axis=0)
    weighted_values = (
        jnp.exp(log_weight - block_max[None, :])[:, :, None] * keys_blk.astype(jnp.float32)
    ).astype(jnp.bfloat16)
    state_total_sum = jnp.einsum(
        "yij,yip->ijp", weighted_values, values_block, preferred_element_type=jnp.float32
    )
    return (running, (state_total_sum, block_max, final_cum))


def block_output(query_block, keys_blk, values_block, in_blk, running, prefix):
    prefix_state = prefix[0]
    prefix_max = prefix[1]
    scores = jnp.einsum("thk,shk->hts", query_block, keys_blk, preferred_element_type=jnp.float32)
    cum_rows = running.T
    input_rows = in_blk.astype(jnp.float32).T
    log_weight = cum_rows[:, :, None] - cum_rows[:, None, :] + input_rows[:, None, :]
    span_rows = running.shape[0]
    causal = lax.broadcasted_iota(jnp.int32, (span_rows, span_rows), 0) >= lax.broadcasted_iota(
        jnp.int32, (span_rows, span_rows), 1
    )
    log_weight = jnp.where(causal[None], log_weight, -jnp.inf)
    carried = cum_rows + prefix_max[:, None]
    row_max = jnp.maximum(carried, jnp.max(log_weight, axis=2))
    mixed_weights = (scores * jnp.exp(log_weight - row_max[:, :, None])).astype(jnp.bfloat16)
    within = jnp.einsum(
        "hts,shv->thv", mixed_weights, values_block, preferred_element_type=jnp.float32
    )
    preceding_portion = jnp.einsum(
        "ydw,dwl->ydl",
        query_block,
        prefix_state.astype(jnp.bfloat16),
        preferred_element_type=jnp.float32,
    )
    return within + jnp.exp(carried - row_max).T[:, :, None] * preceding_portion


def local(queries, key_rows, values, in_gate, forget_gate, out_gate, norm_gain):
    moved = (
        lax.all_to_all(queries, "head", split_axis=1, concat_axis=0, tiled=True),
        lax.all_to_all(key_rows, "head", split_axis=1, concat_axis=0, tiled=True),
        lax.all_to_all(values, "head", split_axis=1, concat_axis=0, tiled=True),
        lax.all_to_all(in_gate, "head", split_axis=1, concat_axis=0, tiled=True),
        lax.all_to_all(forget_gate, "head", split_axis=1, concat_axis=0, tiled=True),
        lax.all_to_all(out_gate, "head", split_axis=1, concat_axis=0, tiled=True),
    )
    gate_rows = moved[5]
    heads_here = moved[3].shape[1]
    total_rows = moved[0].shape[0]
    key_width = moved[0].shape[1] // heads_here
    value_width = moved[2].shape[1] // heads_here
    blocks = total_rows // STRETCH
    query_all = moved[0].reshape(blocks, STRETCH, heads_here, key_width)
    keys_all = moved[1].reshape(blocks, STRETCH, heads_here, key_width)
    values_all = moved[2].reshape(blocks, STRETCH, heads_here, value_width)
    input_all = moved[3].reshape(blocks, STRETCH, heads_here)
    forget_all = moved[4].reshape(blocks, STRETCH, heads_here)
    index_blk = 0
    running, summary = summarize(
        keys_all[index_blk], values_all[index_blk], input_all[index_blk], forget_all[index_blk]
    )
    running_list = [running]
    identity = (
        jnp.zeros((heads_here, key_width, value_width), jnp.float32),
        jnp.full((heads_here,), far_below, jnp.float32),
        jnp.zeros((heads_here,), jnp.float32),
    )
    prefix = prefix_2(summary, "seq", combine, identity)
    index_blk = 0
    mixed_blk = block_output(
        query_all[index_blk],
        keys_all[index_blk],
        values_all[index_blk],
        input_all[index_blk],
        running_list[index_blk],
        prefix,
    )
    mean_sq = jnp.mean(mixed_blk * mixed_blk, axis=-1, keepdims=True)
    normed = (
        mixed_blk * lax.rsqrt(mean_sq + norm_eps) * norm_gain.reshape(heads_here, value_width)
    ).astype(jnp.bfloat16)
    normed = normed.reshape(total_rows, heads_here * value_width)
    gated = (jax.nn.sigmoid(gate_rows.astype(jnp.float32)) * normed.astype(jnp.float32)).astype(
        jnp.bfloat16
    )
    return lax.all_to_all(gated, "head", split_axis=0, concat_axis=1, tiled=True)


def solution(mesh):
    placed = (
        P(("seq", "head"), None),
        P(("seq", "head"), None),
        P(("seq", "head"), None),
        P(("seq", "head"), None),
        P(("seq", "head"), None),
        P(("seq", "head"), None),
        P("head"),
    )
    return jax.shard_map(
        local, mesh=mesh, in_specs=placed, out_specs=P(("seq", "head"), None), check_vma=False
    )
```

profile of v0, /device:TPU:27, one launch (start us, length us, event | category | flops | bytes accessed | tf_op | source)
XLA Modules:
  0.0 439.4 jit_solution(12269905239405438814)
XLA Ops:
  22.3 3.8 all-to-all-start.2
  26.1 4.8 %copy.100 = bf16[64,2,8,2048]{3,2,0,1:T(8,128)(2,1)} copy(bf16[64,2,8,2048]{3,2,1,0:T(8,128)(2,1)} %bitcast.114) | data formatting | bytes 8388608 | tf_op jit(solution)/shard_map/all_to_all | solution.py:84
  30.9 18.3 %all-to-all-done.2 = bf16[512,2,1024]{2,0,1:T(8,128)(2,1)S(1)} async-done(((bf16[512,2,1024]{2,0,1:T(8,128)(2,1)}), bf16[512,2,1024]{2,0,1:T(8,128)(2,1)S(1)}, u32[]{:S(2)}, u32[]{:S(2)}) %all-to-all-start.2) | async-done | bytes 2097184 | tf_op jit(solution)/shard_map/all_to_all | solution.py:83
  50.5 5.6 %all-to-all-start.5 = ((bf16[512,2,2048]{2,0,1:T(8,128)(2,1)}), bf16[512,2,2048]{2,0,1:T(8,128)(2,1)}, u32[]{:S(2)}, u32[]{:S(2)}) async-start(bf16[512,2,2048]{2,0,1:T(8,128)(2,1)} %bitcast.106), calls=%async_computation.5 | async-start | bytes 8388608 | tf_op jit(solution)/shard_map/all_to_all | solution.py:84
  58.5 3.3 squeeze_reshape.12
  64.1 36.8 %all-to-all-done.5 = bf16[512,2,2048]{2,0,1:T(8,128)(2,1)} async-done(((bf16[512,2,2048]{2,0,1:T(8,128)(2,1)}), bf16[512,2,2048]{2,0,1:T(8,128)(2,1)}, u32[]{:S(2)}, u32[]{:S(2)}) %all-to-all-start.5) | async-done | bytes 4194336 | tf_op jit(solution)/shard_map/all_to_all | solution.py:84
  100.9 7.8 %squeeze_reshape.13 = bf16[1024,4,512]{2,1,0:T(4,128)(2,1)} reshape(bf16[2,512,2048]{2,1,0:T(8,128)(2,1)} %bitcast.20) | data formatting | bytes 8388608 | tf_op jit(solution)/shard_map/squeeze;reshape | solution.py:115
  108.7 7.5 %copy.65 = bf16[1024,4,512]{0,2,1:T(8,128)(2,1)} copy(bf16[1024,4,512]{2,1,0:T(4,128)(2,1)} %squeeze_reshape.13) | data formatting | bytes 8388608 | tf_op jit(solution)/shard_map/squeeze;reshape | solution.py:115
  116.2 5.7 %fusion.9 = f32[4,256,512]{2,1,0:T(8,128)} fusion(bf16[1024,4,512]{0,2,1:T(8,128)(2,1)} %copy.65, bf16[1024,4,256]{2,1,0:T(4,128)(2,1)} %multiply_convert_fusion.2), kind=kOutput, calls=%fused_computation.24 | convolution fusion | flops 1073741824 | bytes 8388608 | tf_op jit(solution)/shard_map/yij,yip->ijp/dot_general | solution.py:47
  123.5 3.8 all-to-all-start.1
  127.4 6.6 %copy.51 = bf16[512,4096]{0,1:T(8,128)(2,1)} copy(bf16[512,4096]{1,0:T(8,128)(2,1)} %param.14) | data formatting | bytes 8388608 | tf_op args[5]
  136.7 30.6 %all-reduce = f32[64]{0:T(128)S(1)} all-reduce(f32[64]{0:T(128)S(1)} %dynamic-update-slice), channel_id=2, replica_groups=mesh['seq'=16,'head'=2] {'seq'}, use_global_device_ids=true, to_apply=%add | all-reduce | flops 64 | bytes 512
  167.6 20.2 %all-gather.2 = f32[16,1,4]{2,1,0:T(1,128)S(1)} all-gather(f32[1,1,4]{2,1,0:T(1,128)S(1)} %get-tuple-element.111), channel_id=1, replica_groups=mesh['seq'=16,'head'=2] {'seq'}, dimensions={0}, use_global_device_ids=true | all-gather | bytes 272 | tf_op jit(solution)/shard_map/all_gather | solution.py:15
  187.8 5.2 %fusion.5 = f32[4,1024]{1,0:T(4,128)S(1)} fusion(f32[4,1024]{1,0:T(4,128)S(1)} %copy.58, f32[4,1024]{1,0:T(4,128)S(1)} %bitcast.118, pred[1024,1024]{1,0:T(8,128)(4,1)} %iota_compare_fusion), kind=kLoop, calls=%fused_computation.12 | loop fusion | flops 16773120 | bytes 1097728 | tf_op jit(solution)/shard_map/reduce_max | solution.py:66
  193.0 5.8 %all-to-all-start = ((bf16[512,2,2048]{0,2,1:T(8,128)(2,1)}), bf16[512,2,2048]{0,2,1:T(8,128)(2,1)}, u32[]{:S(2)}, u32[]{:S(2)}) async-start(bf16[512,2,2048]{0,2,1:T(8,128)(2,1)} %bitcast.105), calls=%async_computation | async-start | bytes 8388608 | tf_op jit(solution)/shard_map/all_to_all | solution.py:87
  201.5 91.4 %all-gather.5.cloned.1.call-done = f32[64,256,512]{2,1,0:T(8,128)} async-done(((f32[4,256,512]{2,1,0:T(8,128)}), f32[64,256,512]{2,1,0:T(8,128)}) %all-gather.5.cloned.1.call-update) | async-done | bytes 33554448 | tf_op jit(solution)/shard_map/all_gather | solution.py:15
  293.2 39.9 %while.14 = (s32[]{:T(128)}, f32[4,256,512]{2,1,0:T(8,128)S(1)}, f32[4]{0:T(128)S(1)}, s32[]{:T(128)}, f32[16,4]{1,0:T(8,128)S(1)}, /*index=5*/f32[16,4]{1,0:T(8...) while((s32[]{:T(128)}, f32[4,256,512]{2,1,0:T(8,128)S(1)}, f32[4]{0:T(128)S(1)}, ...), condition=%wide.region_4.5_spmd, body=%wide.region_3.4_spmd.sunk | while | flops 1572885 | bytes 6291763 | solution.py:23
  333.3 14.9 %fusion.13 = f32[4,1024,512]{1,2,0:T(8,128)} fusion(bf16[1024,4,512]{0,2,1:T(8,128)(2,1)} %copy.65, f32[4,1024]{1,0:T(4,128)S(1)} %get-tuple-element.113, f32[4,1024]{1,0:T(4,128)S(1)} %copy.58, f32[4,1024]{1,0:T(4,128)S(1)} %bitcast.119, pred[1024,1024]{1,0:T(8,128)(4,1)S(1)} %copy-done.2, bf16[1024,4,256]{2,1,0:T(4,128)(2,1)} %copy-done, ...), kind=kOutput, calls=%fused_computation.27 | convolution fusion | flops 6467616768 | bytes 17874944 | tf_op jit(solution)/shard_map/hts,shv->thv/dot_general | solution.py:68
  348.2 6.2 %multiply_reduce_fusion = (f32[1024,4]{0,1:T(4,128)S(1)}, f32[1024,4,512]{0,2,1:T(8,128)S(1)}) fusion(bf16[1024,4,256]{2,1,0:T(4,128)(2,1)} %squeeze_reshape.11, f32[4,256,512]{2,1,0:T(8,128)S(1)} %get-tuple-element.65, f32[1024,4]{0,1:T(4,128)S(1)} %get-tuple-element.112, f32[4,1024,512]{1,2,0:T(8,128)} %fusion.13), kind=kOutput, calls=%fused_computation.18 | convolution fusion | flops 1082650624 | bytes 21004288 | tf_op jit(solution)/shard_map/ydw,dwl->ydl/dot_general | solution.py:71
  354.4 4.0 fusion.8
  358.4 11.8 %reshape.113 = f32[2,512,2048]{1,0,2:T(2,128)} reshape(f32[1024,4,512]{0,2,1:T(8,128)} %fusion.8) | data formatting | bytes 16777216 | tf_op jit(solution)/shard_map/convert_element_type | solution.py:125
  370.2 6.7 %fusion.7 = bf16[2,512,2048]{1,2,0:T(8,128)(2,1)S(1)} fusion(f32[2,512,2048]{1,0,2:T(2,128)} %reshape.113, bf16[512,2,2048]{0,2,1:T(8,128)(2,1)} %all-to-all-done), kind=kLoop, calls=%fused_computation.16 | loop fusion | flops 12582912 | bytes 16777216 | tf_op jit(solution)/shard_map/convert_element_type | solution.py:125
  376.8 49.4 %all_to_all.103 = bf16[2,512,2048]{1,2,0:T(8,128)(2,1)} all-to-all(bf16[2,512,2048]{1,2,0:T(8,128)(2,1)S(1)} %fusion.7), channel_id=1, replica_groups=mesh['seq'=16,'head'=2] {'head'}, dimensions={0} | all-to-all | bytes 8388608 | tf_op jit(solution)/shard_map/all_to_all | solution.py:128
  426.2 6.3 %copy.69 = bf16[512,4096]{1,0:T(8,128)(2,1)} copy(bf16[512,4096]{0,1:T(8,128)(2,1)} %bitcast.107) | data formatting | bytes 8388608 | tf_op jit(solution)/shard_map/all_to_all | solution.py:128
  (97 shorter events, 67.9 us)
Async XLA Ops:
  7.8 5.9 %all-to-all-start.3 = ((bf16[512,2,4]{0,2,1:T(4,128)(2,1)}), bf16[512,2,4]{0,2,1:T(4,128)(2,1)S(1)}, u32[]{:S(2)}, u32[]{:S(2)}) async-start(bf16[512,2,4]{0,2,1:T(4,128)(2,1)} %all_to_all.86), calls=%async_computation.3 | async-start | bytes 16384 | tf_op jit(solution)/shard_map/all_to_all | solution.py:86
  13.7 8.6 %all-to-all-start.4 = ((bf16[512,2,4]{0,2,1:T(4,128)(2,1)}), bf16[512,2,4]{0,2,1:T(4,128)(2,1)S(1)}, u32[]{:S(2)}, u32[]{:S(2)}) async-start(bf16[512,2,4]{0,2,1:T(4,128)(2,1)} %all_to_all.88), calls=%async_computation.4 | async-start | bytes 16384 | tf_op jit(solution)/shard_map/all_to_all | solution.py:85
  22.3 26.9 %all-to-all-start.2 = ((bf16[512,2,1024]{2,0,1:T(8,128)(2,1)}), bf16[512,2,1024]{2,0,1:T(8,128)(2,1)S(1)}, u32[]{:S(2)}, u32[]{:S(2)}) async-start(bf16[512,2,1024]{2,0,1:T(8,128)(2,1)} %copy.54), calls=%async_computation.2 | async-start | bytes 4194304 | tf_op jit(solution)/shard_map/all_to_all | solution.py:83
  49.2 1.3 copy-start.1
  50.5 50.4 %all-to-all-start.5 = ((bf16[512,2,2048]{2,0,1:T(8,128)(2,1)}), bf16[512,2,2048]{2,0,1:T(8,128)(2,1)}, u32[]{:S(2)}, u32[]{:S(2)}) async-start(bf16[512,2,2048]{2,0,1:T(8,128)(2,1)} %bitcast.106), calls=%async_computation.5 | async-start | bytes 8388608 | tf_op jit(solution)/shard_map/all_to_all | solution.py:84
  56.1 236.8 %all-gather.5.cloned.1.call-start = ((), (), s32[]{:S(2)}) async-start(), calls=%async_computation.7 | async-start | bytes 35651584 | tf_op jit(solution)/shard_map/all_gather | solution.py:15
  61.9 46.9 %copy-start = (bf16[1024,4,256]{2,1,0:T(4,128)(2,1)}, bf16[1024,4,256]{2,1,0:T(4,128)(2,1)S(1)}, u32[]{:S(2)}) copy-start(bf16[1024,4,256]{2,1,0:T(4,128)(2,1)S(1)} %squeeze_reshape.12) | copy-start | bytes 6291460
  116.2 5.8 %copy-start.3 = (bf16[512,2048]{1,0:T(8,128)(2,1)S(1)}, bf16[512,2048]{1,0:T(8,128)(2,1)}, u32[]{:S(2)}) copy-start(bf16[512,2048]{1,0:T(8,128)(2,1)} %param.9) | copy-start | bytes 6291460
  122.0 5.3 %copy-start.4 = (f32[2048]{0:T(1024)S(1)}, f32[2048]{0:T(1024)}, u32[]{:S(2)}) copy-start(f32[2048]{0:T(1024)} %param.15) | copy-start | bytes 24580
  123.5 69.4 %all-to-all-start.1 = ((bf16[512,2,1024]{2,0,1:T(8,128)(2,1)}), bf16[512,2,1024]{2,0,1:T(8,128)(2,1)S(1)}, u32[]{:S(2)}, u32[]{:S(2)}) async-start(bf16[512,2,1024]{2,0,1:T(8,128)(2,1)} %bitcast.110), calls=%async_computation.1 | async-start | bytes 4194304 | tf_op jit(solution)/shard_map/all_to_all | solution.py:82
  127.3 6.6 %copy-start.5 = (u32[32]{0:T(128)S(1)}, u32[32]{0:T(128)}, u32[]{:S(2)}) copy-start(u32[32]{0:T(128)} %constant.48) | copy-start | bytes 388
  193.0 177.2 %all-to-all-start = ((bf16[512,2,2048]{0,2,1:T(8,128)(2,1)}), bf16[512,2,2048]{0,2,1:T(8,128)(2,1)}, u32[]{:S(2)}, u32[]{:S(2)}) async-start(bf16[512,2,2048]{0,2,1:T(8,128)(2,1)} %bitcast.105), calls=%async_computation | async-start | bytes 8388608 | tf_op jit(solution)/shard_map/all_to_all | solution.py:87
  293.2 40.1 %copy-start.2 = (pred[1024,1024]{1,0:T(8,128)(4,1)S(1)}, pred[1024,1024]{1,0:T(8,128)(4,1)}, u32[]{:S(2)}) copy-start(pred[1024,1024]{1,0:T(8,128)(4,1)} %iota_compare_fusion) | copy-start | bytes 3145732
Sparse Core Ops, SparseCore 0:
  122.1 170.7 all-gather.4
where the time goes:
time: 441 us; the launch traced here: 439 us
  waiting for transfers between devices  148 us (34%)
  blocking collectives  100 us (23%)
  local copies, waits for them, and re-layouts  63.7 us (14%)
  other arithmetic  60.4 us (14%)
  matrix products  26.8 us (6%)
  starting transfers between devices  25.4 us (6%)
  between operations  14.3 us (3%)
    all_gather x1, waiting for transfers between devices, prefix_2(): gathered = jax.tree.map(lambda a: lax.all_gather(a, axis), part)  91.4 us
    all_to_all x1, blocking collectives, local(): lax.all_to_all(gated, 'head', split_axis=0, concat_axis=1, tiled=True)  49.4 us
    add x15, other arithmetic, combine(): jnp.exp(shifted - joint_max)[..., None, None] * state_a  38.7 us
    all_to_all x1, waiting for transfers between devices, local(): lax.all_to_all(values, 'head', split_axis=1, concat_axis=0, tiled=True)  36.8 us
    unnamed x1, blocking collectives  30.6 us
    all_gather x1, blocking collectives, prefix_2(): gathered = jax.tree.map(lambda a: lax.all_gather(a, axis), part)  20.2 us
    all_to_all x1, waiting for transfers between devices, local(): lax.all_to_all(key_rows, 'head', split_axis=1, concat_axis=0, tiled=True)  18.3 us
    another operation x2, local copies, waits for them, and re-layouts, local(): values_all[index_blk]  15.3 us
  transfers between devices with their start and end apart: 7, of which 4 were waited for; matrix products, arithmetic and copies ran while one was open for 26% of the time, Pallas kernels for 0%

commit v1 on v0

v1 whole, which is shorter than its diff:
```python
import functools

import jax
import jax.numpy as jnp
from jax import lax
from jax.experimental import pallas as pl
from jax.experimental.pallas import tpu as pltpu

far_below = -1e30
norm_eps = 1e-06
MESH = pl.DeviceIdType.MESH
F32 = jnp.float32
BF16 = jnp.bfloat16
PIECES = 2


def kernel(
    n, m, H, NP,
    q_hbm, k_hbm, v_hbm, ig_ref, fg_ref, igt_ref, fgt_ref, og_hbm, gain_ref,
    out_hbm,
    q, k, v, og, ob, within, acol, arow, dec, amax, scal_s, scal, mall, e1, e2, alph,
    cm, gain, sb, rb, dbuf, cs, cr, pb, pr,
    in_sem, out_sem, scs, scr, cms, cmr, gs, gr, s1, r1, sc, rc, s3, r3,
):
    T, HK = q.shape
    DK = HK // H
    DV = v.shape[1] // H
    c = H // m
    nA = n // c
    RP = DK // NP
    a = lax.axis_index("seq")
    b = lax.axis_index("head")
    A = a // c
    l = (a % c) * m + b

    loads = [
        pltpu.make_async_copy(src, dst, in_sem.at[i])
        for i, (src, dst) in enumerate(((k_hbm, k), (v_hbm, v), (q_hbm, q), (og_hbm, og)))
    ]
    for ld in loads:
        ld.start()

    def member(lp):
        return (A * c + lp // m, lp % m)

    def other(o):
        return (l + o) % H

    has_prev = A > 0
    has_next = A < nA - 1

    barrier = pltpu.get_barrier_semaphore()
    for o in range(1, H):
        pl.semaphore_signal(barrier, inc=1, device_id=member(other(o)), device_id_type=MESH)

    @pl.when(has_prev)
    def _():
        pl.semaphore_signal(barrier, inc=1, device_id=(a - c, b), device_id_type=MESH)

    @pl.when(has_next)
    def _():
        pl.semaphore_signal(barrier, inc=1, device_id=(a + c, b), device_id_type=MESH)

    rows_i = lax.broadcasted_iota(jnp.int32, (T, T), 0)
    cols_i = lax.broadcasted_iota(jnp.int32, (T, T), 1)
    lower = (rows_i >= cols_i).astype(F32)
    upper = (rows_i <= cols_i).astype(F32)
    lf_col = jax.nn.log_sigmoid(fg_ref[...].astype(F32))
    lf_row = jax.nn.log_sigmoid(fgt_ref[...].astype(F32))
    cum_col = jnp.dot(lower, lf_col, precision=lax.Precision.HIGHEST, preferred_element_type=F32)
    cum_row = jnp.dot(lf_row, upper, precision=lax.Precision.HIGHEST, preferred_element_type=F32)
    a_col = ig_ref[...].astype(F32) - cum_col
    a_row = igt_ref[...].astype(F32) - cum_row
    for h in range(H):
        acol[h] = a_col[:, h : h + 1]
    arow[...] = a_row
    top = jnp.broadcast_to(jnp.max(a_row, axis=1, keepdims=True), (H, 128))
    total = jnp.broadcast_to(cum_row[:, T - 1 : T], (H, 128))
    amax[...] = top
    scal_s[0] = total + top
    scal_s[1] = total
    scal[l, 0] = total + top
    scal[l, 1] = total
    gain[b] = gain_ref[...]

    pl.semaphore_wait(barrier, H - 1 + has_prev.astype(jnp.int32) + has_next.astype(jnp.int32))

    def scal_copy(o, src):
        return pltpu.make_async_remote_copy(
            src_ref=scal_s, dst_ref=scal.at[src], send_sem=scs.at[o], recv_sem=scr.at[src],
            device_id=member(other(o)), device_id_type=MESH)

    def gain_copy(o, src):
        return pltpu.make_async_remote_copy(
            src_ref=gain_ref, dst_ref=gain.at[src], send_sem=gs.at[o], recv_sem=gr.at[src],
            device_id=(a, (b + o) % m), device_id_type=MESH)

    def sum_copy(o, p, src):
        rows = pl.ds(p * RP, RP)
        return pltpu.make_async_remote_copy(
            src_ref=sb.at[other(o), rows], dst_ref=rb.at[src, rows],
            send_sem=s1.at[o, p], recv_sem=r1.at[src, p],
            device_id=member(other(o)), device_id_type=MESH)

    def pre_copy(o, p, src):
        rows = pl.ds(p * RP, RP)
        return pltpu.make_async_remote_copy(
            src_ref=pb.at[other(o), rows], dst_ref=pr.at[src, rows],
            send_sem=s3.at[o, p], recv_sem=r3.at[src, p],
            device_id=member(other(o)), device_id_type=MESH)

    def chain_copy(p):
        rows = pl.ds(p * RP, RP)
        return pltpu.make_async_remote_copy(
            src_ref=cs.at[rows], dst_ref=cr.at[rows], send_sem=sc.at[p], recv_sem=rc.at[p],
            device_id=(a + c, b), device_id_type=MESH)

    def max_copy():
        return pltpu.make_async_remote_copy(
            src_ref=mall.at[H], dst_ref=cm, send_sem=cms, recv_sem=cmr,
            device_id=(a + c, b), device_id_type=MESH)

    for o in range(1, H):
        scal_copy(o, l).start()
    for o in range(1, m):
        gain_copy(o, b).start()

    loads[0].wait()
    loads[1].wait()

    def summary(h):
        kc = pl.ds(pl.multiple_of(h * DK, DK), DK)
        vc = pl.ds(pl.multiple_of(h * DV, DV), DV)
        w = jnp.exp(acol[h] - amax[pl.ds(h, 1), 0:1])
        wk = (w * k[:, kc].astype(F32)).astype(BF16)
        return lax.dot_general(
            wk, v[:, vc], (((0,), (0,)), ((), ())), preferred_element_type=F32
        ).astype(BF16)

    def first_piece(o, carry):
        sb[other(o)] = summary(other(o))
        sum_copy(o, 0, l).start()
        return carry

    lax.fori_loop(1, H, first_piece, 0)
    for p in range(1, NP):
        for o in range(1, H):
            sum_copy(o, p, l).start()
    rb[l] = summary(l)

    for o in range(1, H):
        scal_copy(o, other(o)).wait_recv()

    @pl.when(has_prev)
    def _():
        max_copy().wait_recv()
        mall[0] = cm[...]

    @pl.when(jnp.logical_not(has_prev))
    def _():
        mall[0] = jnp.full((H, 128), far_below, F32)

    al = jnp.ones((H, 128), F32)
    before = mall[0]
    alph[0] = al
    for i in range(H):
        own, decay = scal[i, 0], scal[i, 1]
        shifted = before + decay
        after = jnp.maximum(shifted, own)
        x1 = jnp.exp(shifted - after)
        e1[i] = x1
        e2[i] = jnp.exp(own - after)
        al = al * x1
        alph[i + 1] = al
        mall[i + 1] = after
        before = after

    @pl.when(has_next)
    def _():
        max_copy().start()

    loads[2].wait()
    TB = min(256, T)

    def inner(h, carry):
        kc = pl.ds(pl.multiple_of(h * DK, DK), DK)
        vc = pl.ds(pl.multiple_of(h * DV, DV), DV)
        M = mall[l, pl.ds(h, 1), 0:1]
        for t0 in range(0, T, TB):
            S = t0 + TB
            row = arow[pl.ds(h, 1), 0:S]
            causal = (lax.broadcasted_iota(jnp.int32, (TB, S), 0) + t0) >= (
                lax.broadcasted_iota(jnp.int32, (TB, S), 1))
            lw = jnp.where(causal, jnp.broadcast_to(row, (TB, S)), -jnp.inf)
            r = jnp.maximum(jnp.max(lw, axis=1, keepdims=True), M)
            sco = lax.dot_general(
                q[t0 : t0 + TB, kc], k[0:S, kc], (((1,), (1,)), ((), ())),
                preferred_element_type=F32)
            mix = (sco * jnp.exp(lw - r)).astype(BF16)
            within[t0 : t0 + TB, vc] = jnp.dot(mix, v[0:S, vc], preferred_element_type=F32)
            dec[h, t0 : t0 + TB] = jnp.exp(M - r)
        return carry

    lax.fori_loop(0, H, inner, 0)

    for p in range(NP):
        rows = slice(p * RP, (p + 1) * RP)
        for o in range(1, H):
            sum_copy(o, p, other(o)).wait_recv()
        one = pl.ds(l, 1)
        dbuf[0] = jnp.zeros((RP, DV), F32)
        for i in range(H):
            dbuf[i + 1] = e1[i, one, 0:1] * dbuf[i] + e2[i, one, 0:1] * rb[i, rows].astype(F32)

        @pl.when(has_prev)
        def _():
            chain_copy(p).wait_recv()

        @pl.when(jnp.logical_not(has_prev))
        def _():
            cr[rows] = jnp.zeros((RP, DV), BF16)

        @pl.when(has_next)
        def _():
            cs[rows] = (alph[H, one, 0:1] * cr[rows].astype(F32) + dbuf[H]).astype(BF16)
            chain_copy(p).start()

        for i in range(H):
            pb[i, rows] = (alph[i, one, 0:1] * cr[rows].astype(F32) + dbuf[i]).astype(BF16)
        for o in range(1, H):
            pre_copy(o, p, l).start()
        pr[l, rows] = pb[l, rows]

    loads[3].wait()
    for o in range(1, m):
        gain_copy(o, (b + o) % m).wait_recv()

    def out_copy(h):
        vc = pl.ds(pl.multiple_of(h * DV, DV), DV)
        return pltpu.make_async_copy(ob.at[:, vc], out_hbm.at[:, vc], out_sem.at[h])

    def finish(o, carry):
        h = other(o)

        @pl.when(o > 0)
        def _():
            for p in range(NP):
                pre_copy(o, p, h).wait_recv()

        kc = pl.ds(pl.multiple_of(h * DK, DK), DK)
        vc = pl.ds(pl.multiple_of(h * DV, DV), DV)
        g = gain[h // c, :, pl.ds(pl.multiple_of((h % c) * DV, DV), DV)]
        for t0 in range(0, T, TB):
            ts = slice(t0, t0 + TB)
            early = jnp.dot(q[ts, kc], pr[h], preferred_element_type=F32)
            mixed = within[ts, vc] + dec[h, ts] * early
            ms = jnp.mean(mixed * mixed, axis=1, keepdims=True)
            normed = (mixed * lax.rsqrt(ms + norm_eps) * g).astype(BF16)
            gate = jax.nn.sigmoid(og[ts, vc].astype(F32))
            ob[ts, vc] = (gate * normed.astype(F32)).astype(BF16)
        out_copy(h).start()
        return carry

    lax.fori_loop(0, H, finish, 0)

    for h in range(H):
        out_copy(h).wait()
    for o in range(1, H):
        scal_copy(o, l).wait_send()
        for p in range(NP):
            sum_copy(o, p, l).wait_send()
            pre_copy(o, p, l).wait_send()
    for o in range(1, m):
        gain_copy(o, b).wait_send()

    @pl.when(has_next)
    def _():
        max_copy().wait_send()
        for p in range(NP):
            chain_copy(p).wait_send()


def local(n, m, queries, key_rows, values, in_gate, forget_gate, out_gate, norm_gain):
    T, H = in_gate.shape
    HK = queries.shape[1]
    HV = values.shape[1]
    DK, DV = HK // H, HV // H
    NP = PIECES
    RP = DK // NP
    any_ = pl.BlockSpec(memory_space=pl.ANY)
    vm = pl.BlockSpec(memory_space=pltpu.VMEM)
    V = pltpu.VMEM
    D = pltpu.SemaphoreType.DMA
    gain2 = norm_gain.reshape(1, -1)
    return pl.pallas_call(
        functools.partial(kernel, n, m, H, NP),
        out_shape=jax.ShapeDtypeStruct((T, HV), BF16),
        in_specs=[any_, any_, any_, vm, vm, vm, vm, any_, vm],
        out_specs=any_,
        scratch_shapes=[
            V((T, HK), BF16), V((T, HK), BF16), V((T, HV), BF16), V((T, HV), BF16),
            V((T, HV), BF16), V((T, HV), F32),
            V((H, T, 1), F32), V((H, T), F32), V((H, T, 1), F32), V((H, 128), F32),
            V((2, H, 128), F32), V((H, 2, H, 128), F32), V((H + 1, H, 128), F32),
            V((H, H, 128), F32), V((H, H, 128), F32), V((H + 1, H, 128), F32),
            V((H, 128), F32), V((m, 1, gain2.shape[1]), F32),
            V((H, DK, DV), BF16), V((H, DK, DV), BF16), V((H + 1, RP, DV), F32),
            V((DK, DV), BF16), V((DK, DV), BF16), V((H, DK, DV), BF16), V((H, DK, DV), BF16),
            D((4,)), D((H,)), D((H,)), D((H,)), D, D, D((m,)), D((m,)),
            D((H, NP)), D((H, NP)), D((NP,)), D((NP,)), D((H, NP)), D((H, NP)),
        ],
        compiler_params=pltpu.CompilerParams(
            collective_id=0, has_side_effects=True, vmem_limit_bytes=60 * 1024 * 1024),
    )(queries, key_rows, values, in_gate, forget_gate, in_gate.T, forget_gate.T, out_gate, gain2)


def solution(mesh):
    row = jax.sharding.PartitionSpec(("seq", "head"), None)
    n, m = mesh.shape["seq"], mesh.shape["head"]
    return jax.shard_map(
        functools.partial(local, n, m), mesh=mesh,
        in_specs=(row,) * 6 + (jax.sharding.PartitionSpec("head"),),
        out_specs=row, check_vma=False,
    )
```

time: 441 us -> 70.7 us (0.16)
  the two profiles are of different devices: /device:TPU:27 before, /device:TPU:29 now
where the time goes in v1:
time: 70.7 us; the launch traced here: 70.5 us
  Pallas kernels  62.8 us (89%)
  local copies, waits for them, and re-layouts  7.66 us (11%)
    pallas_call x1, Pallas kernels, local(): pl.pallas_call(functools.partial(kernel, n, m, H, NP), out_shape=jax.Shap...  62.8 us
    unnamed x3, local copies, waits for them, and re-layouts  7.66 us

profile of v1, /device:TPU:29, one launch (start us, length us, event | category | flops | bytes accessed | tf_op | source)
XLA Modules:
  0.0 70.5 jit_solution(6723698619868070527)
XLA Ops:
  0.0 1.5 %copy.8.ig_ref = bf16[512,8]{1,0:T(8,128)(2,1)} copy(bf16[512,8]{0,1:T(8,128)(2,1)} %param.10) | data formatting | bytes 16384 | tf_op args[3]
  1.5 1.5 %copy.9.fg_ref = bf16[512,8]{1,0:T(8,128)(2,1)} copy(bf16[512,8]{0,1:T(8,128)(2,1)} %param.11) | data formatting | bytes 16384 | tf_op args[4]
  3.0 62.8 %shard_map.73 = bf16[512,4096]{1,0:T(8,128)(2,1)} custom-call(bf16[512,2048]{1,0:T(8,128)(2,1)} %q_hbm.1, bf16[512,2048]{1,0:T(8,128)(2,1)} %k_hbm.1, bf16[512,4096]{1,0:T(8,128)(2,1)} %v_hbm.1, bf16[512,8]{1,0:T(8,128)(2,1)} %copy.8.ig_ref, bf16[512,8]{1,0:T(8,128)(2,1)} %copy.9.fg_ref, bf16[8,512]{1,0:T(8,128)(2,1)} %bitcast.3, bf16[8,512]{1,0:T(8,128)(2,1)} %bitcast.4, ...), custom_call_target="tpu_custom_call" | custom-call | tf_op jit(solution)/shard_map/pallas_call | solution.py:295
  65.8 4.7 %copy.11 = bf16[512,4096]{1,0:T(8,128)(2,1)} copy(bf16[512,4096]{1,0:T(8,128)(2,1)} %shard_map.73) | data formatting | bytes 8388608

commit v2 on v1

--- a/solution.py
+++ b/solution.py
@@ -11,16 +11,17 @@
 MESH = pl.DeviceIdType.MESH
 F32 = jnp.float32
 BF16 = jnp.bfloat16
-PIECES = 2
+PIECES = 4
+AHEAD = 2
 
 
 def kernel(
     n, m, H, NP,
-    q_hbm, k_hbm, v_hbm, ig_ref, fg_ref, igt_ref, fgt_ref, og_hbm, gain_ref,
+    q_hbm, k_hbm, v_hbm, igt_ref, fgt_ref, gain_ref,
     out_hbm,
-    q, k, v, og, ob, within, acol, arow, dec, amax, scal_s, scal, mall, e1, e2, alph,
+    q, k, v, ob, within, acol, arow, dec, amax, scal_s, scal, mall, e1, e2, alph,
     cm, gain, sb, rb, dbuf, cs, cr, pb, pr,
-    in_sem, out_sem, scs, scr, cms, cmr, gs, gr, s1, r1, sc, rc, s3, r3,
+    in_sem, kv_sem, out_sem, scs, scr, cms, cmr, gs, gr, s1, r1, sc, rc, s3, r3,
 ):
     T, HK = q.shape
     DK = HK // H
@@ -33,18 +34,26 @@
     A = a // c
     l = (a % c) * m + b
 
-    loads = [
-        pltpu.make_async_copy(src, dst, in_sem.at[i])
-        for i, (src, dst) in enumerate(((k_hbm, k), (v_hbm, v), (q_hbm, q), (og_hbm, og)))
-    ]
-    for ld in loads:
-        ld.start()
-
     def member(lp):
         return (A * c + lp // m, lp % m)
 
     def other(o):
         return (l + o) % H
+
+    def head_loads(o):
+        h = other(o)
+        kc = pl.ds(pl.multiple_of(h * DK, DK), DK)
+        vc = pl.ds(pl.multiple_of(h * DV, DV), DV)
+        return (
+            pltpu.make_async_copy(k_hbm.at[:, kc], k.at[:, kc], kv_sem.at[o, 0]),
+            pltpu.make_async_copy(v_hbm.at[:, vc], v.at[:, vc], kv_sem.at[o, 1]),
+        )
+
+    for o in (*range(1, H), 0):
+        for ld in head_loads(o):
+            ld.start()
+    q_load = pltpu.make_async_copy(q_hbm, q, in_sem)
+    q_load.start()
 
     has_prev = A > 0
     has_next = A < nA - 1
@@ -63,14 +72,11 @@
 
     rows_i = lax.broadcasted_iota(jnp.int32, (T, T), 0)
     cols_i = lax.broadcasted_iota(jnp.int32, (T, T), 1)
-    lower = (rows_i >= cols_i).astype(F32)
     upper = (rows_i <= cols_i).astype(F32)
-    lf_col = jax.nn.log_sigmoid(fg_ref[...].astype(F32))
     lf_row = jax.nn.log_sigmoid(fgt_ref[...].astype(F32))
-    cum_col = jnp.dot(lower, lf_col, precision=lax.Precision.HIGHEST, preferred_element_type=F32)
     cum_row = jnp.dot(lf_row, upper, precision=lax.Precision.HIGHEST, preferred_element_type=F32)
-    a_col = ig_ref[...].astype(F32) - cum_col
     a_row = igt_ref[...].astype(F32) - cum_row
+    a_col = a_row.T
     for h in range(H):
         acol[h] = a_col[:, h : h + 1]
     arow[...] = a_row
@@ -125,9 +131,6 @@
     for o in range(1, m):
         gain_copy(o, b).start()
 
-    loads[0].wait()
-    loads[1].wait()
-
     def summary(h):
         kc = pl.ds(pl.multiple_of(h * DK, DK), DK)
         vc = pl.ds(pl.multiple_of(h * DV, DV), DV)
@@ -138,6 +141,8 @@
         ).astype(BF16)
 
     def first_piece(o, carry):
+        for ld in head_loads(o):
+            ld.wait()
         sb[other(o)] = summary(other(o))
         sum_copy(o, 0, l).start()
         return carry
@@ -146,6 +151,8 @@
     for p in range(1, NP):
         for o in range(1, H):
             sum_copy(o, p, l).start()
+    for ld in head_loads(0):
+        ld.wait()
     rb[l] = summary(l)
 
     for o in range(1, H):
@@ -179,7 +186,7 @@
     def _():
         max_copy().start()
 
-    loads[2].wait()
+    q_load.wait()
     TB = min(256, T)
 
     def inner(h, carry):
@@ -201,7 +208,7 @@
             dec[h, t0 : t0 + TB] = jnp.exp(M - r)
         return carry
 
-    lax.fori_loop(0, H, inner, 0)
+    lax.fori_loop(0, AHEAD, inner, 0)
 
     for p in range(NP):
         rows = slice(p * RP, (p + 1) * RP)
@@ -231,7 +238,8 @@
             pre_copy(o, p, l).start()
         pr[l, rows] = pb[l, rows]
 
-    loads[3].wait()
+    lax.fori_loop(AHEAD, H, inner, 0)
+
     for o in range(1, m):
         gain_copy(o, (b + o) % m).wait_recv()
 
@@ -240,7 +248,7 @@
         return pltpu.make_async_copy(ob.at[:, vc], out_hbm.at[:, vc], out_sem.at[h])
 
     def finish(o, carry):
-        h = other(o)
+        h = other(H - o)
 
         @pl.when(o > 0)
         def _():
@@ -255,9 +263,7 @@
             early = jnp.dot(q[ts, kc], pr[h], preferred_element_type=F32)
             mixed = within[ts, vc] + dec[h, ts] * early
             ms = jnp.mean(mixed * mixed, axis=1, keepdims=True)
-            normed = (mixed * lax.rsqrt(ms + norm_eps) * g).astype(BF16)
-            gate = jax.nn.sigmoid(og[ts, vc].astype(F32))
-            ob[ts, vc] = (gate * normed.astype(F32)).astype(BF16)
+            ob[ts, vc] = (mixed * lax.rsqrt(ms + norm_eps) * g).astype(BF16)
         out_copy(h).start()
         return carry
 
@@ -292,13 +298,13 @@
     V = pltpu.VMEM
     D = pltpu.SemaphoreType.DMA
     gain2 = norm_gain.reshape(1, -1)
-    return pl.pallas_call(
+    normed = pl.pallas_call(
         functools.partial(kernel, n, m, H, NP),
         out_shape=jax.ShapeDtypeStruct((T, HV), BF16),
-        in_specs=[any_, any_, any_, vm, vm, vm, vm, any_, vm],
+        in_specs=[any_, any_, any_, vm, vm, vm],
         out_specs=any_,
         scratch_shapes=[
-            V((T, HK), BF16), V((T, HK), BF16), V((T, HV), BF16), V((T, HV), BF16),
+            V((T, HK), BF16), V((T, HK), BF16), V((T, HV), BF16),
             V((T, HV), BF16), V((T, HV), F32),
             V((H, T, 1), F32), V((H, T), F32), V((H, T, 1), F32), V((H, 128), F32),
             V((2, H, 128), F32), V((H, 2, H, 128), F32), V((H + 1, H, 128), F32),
@@ -306,12 +312,13 @@
             V((H, 128), F32), V((m, 1, gain2.shape[1]), F32),
             V((H, DK, DV), BF16), V((H, DK, DV), BF16), V((H + 1, RP, DV), F32),
             V((DK, DV), BF16), V((DK, DV), BF16), V((H, DK, DV), BF16), V((H, DK, DV), BF16),
-            D((4,)), D((H,)), D((H,)), D((H,)), D, D, D((m,)), D((m,)),
+            D, D((H, 2)), D((H,)), D((H,)), D((H,)), D, D, D((m,)), D((m,)),
             D((H, NP)), D((H, NP)), D((NP,)), D((NP,)), D((H, NP)), D((H, NP)),
         ],
         compiler_params=pltpu.CompilerParams(
             collective_id=0, has_side_effects=True, vmem_limit_bytes=60 * 1024 * 1024),
-    )(queries, key_rows, values, in_gate, forget_gate, in_gate.T, forget_gate.T, out_gate, gain2)
+    )(queries, key_rows, values, in_gate.T, forget_gate.T, gain2)
+    return (jax.nn.sigmoid(out_gate.astype(F32)) * normed.astype(F32)).astype(BF16)
 
 
 def solution(mesh):

time: 70.7 us -> 61.7 us (0.87)
  the two profiles are of different devices: /device:TPU:29 before, /device:TPU:1 now
where the time goes in v2:
time: 61.7 us; the launch traced here: 61.4 us
  Pallas kernels  55.5 us (90%)
  other arithmetic  5.96 us (10%)
    pallas_call x1, Pallas kernels, local(): pl.pallas_call(functools.partial(kernel, n, m, H, NP), out_shape=jax.Shap...  55.5 us
    convert_element_type x1, other arithmetic, local(): (jax.nn.sigmoid(out_gate.astype(F32)) * normed.astype(F32)).astype(BF16)  5.96 us

profile of v2, /device:TPU:1, one launch (start us, length us, event | category | flops | bytes accessed | tf_op | source)
XLA Modules:
  0.0 61.4 jit_solution(2805618029537534792)
XLA Ops:
  0.0 55.5 %shard_map.73 = bf16[512,4096]{1,0:T(8,128)(2,1)} custom-call(bf16[512,2048]{1,0:T(8,128)(2,1)} %q_hbm.1, bf16[512,2048]{1,0:T(8,128)(2,1)} %k_hbm.1, bf16[512,4096]{1,0:T(8,128)(2,1)} %v_hbm.1, bf16[8,512]{1,0:T(8,128)(2,1)} %bitcast.3, bf16[8,512]{1,0:T(8,128)(2,1)} %bitcast.4, f32[1,2048]{1,0:T(1,128)} %bitcast.5), custom_call_target="tpu_custom_call" | custom-call | tf_op jit(solution)/shard_map/pallas_call | solution.py:301
  55.5 6.0 %multiply_convert_fusion = bf16[512,4096]{1,0:T(8,128)(2,1)} fusion(bf16[512,4096]{1,0:T(8,128)(2,1)} %shard_map.73, bf16[512,4096]{1,0:T(8,128)(2,1)} %param.12), kind=kLoop, calls=%fused_computation | loop fusion | flops 14680064 | bytes 12582912 | tf_op jit(solution)/shard_map/convert_element_type | solution.py:321

commit v3 on v2

--- a/solution.py
+++ b/solution.py
@@ -17,11 +17,11 @@
 
 def kernel(
     n, m, H, NP,
-    q_hbm, k_hbm, v_hbm, igt_ref, fgt_ref, gain_ref,
+    q_hbm, k_hbm, v_hbm, igt_hbm, fgt_hbm, gain_hbm,
     out_hbm,
     q, k, v, ob, within, acol, arow, dec, amax, scal_s, scal, mall, e1, e2, alph,
     cm, gain, sb, rb, dbuf, cs, cr, pb, pr,
-    in_sem, kv_sem, out_sem, scs, scr, cms, cmr, gs, gr, s1, r1, sc, rc, s3, r3,
+    igt_ref, fgt_ref, gain_ref, small_sem, in_sem, kv_sem, out_sem, scs, scr, cms, cmr, gs, gr, s1, r1, sc, rc, s3, r3,
 ):
     T, HK = q.shape
     DK = HK // H
@@ -49,6 +49,13 @@
             pltpu.make_async_copy(v_hbm.at[:, vc], v.at[:, vc], kv_sem.at[o, 1]),
         )
 
+    small = [
+        pltpu.make_async_copy(src, dst, small_sem.at[i])
+        for i, (src, dst) in enumerate(
+            ((fgt_hbm, fgt_ref), (igt_hbm, igt_ref), (gain_hbm, gain_ref)))
+    ]
+    for ld in small:
+        ld.start()
     for o in (*range(1, H), 0):
         for ld in head_loads(o):
             ld.start()
@@ -70,6 +77,8 @@
     def _():
         pl.semaphore_signal(barrier, inc=1, device_id=(a + c, b), device_id_type=MESH)
 
+    for ld in small:
+        ld.wait()
     rows_i = lax.broadcasted_iota(jnp.int32, (T, T), 0)
     cols_i = lax.broadcasted_iota(jnp.int32, (T, T), 1)
     upper = (rows_i <= cols_i).astype(F32)
@@ -301,7 +310,7 @@
     normed = pl.pallas_call(
         functools.partial(kernel, n, m, H, NP),
         out_shape=jax.ShapeDtypeStruct((T, HV), BF16),
-        in_specs=[any_, any_, any_, vm, vm, vm],
+        in_specs=[any_] * 6,
         out_specs=any_,
         scratch_shapes=[
             V((T, HK), BF16), V((T, HK), BF16), V((T, HV), BF16),
@@ -312,12 +321,13 @@
             V((H, 128), F32), V((m, 1, gain2.shape[1]), F32),
             V((H, DK, DV), BF16), V((H, DK, DV), BF16), V((H + 1, RP, DV), F32),
             V((DK, DV), BF16), V((DK, DV), BF16), V((H, DK, DV), BF16), V((H, DK, DV), BF16),
-            D, D((H, 2)), D((H,)), D((H,)), D((H,)), D, D, D((m,)), D((m,)),
+            V((H, T), BF16), V((H, T), BF16), V(gain2.shape, F32), D((3,)), D, D((H, 2)), D((H,)), D((H,)), D((H,)), D, D, D((m,)), D((m,)),
             D((H, NP)), D((H, NP)), D((NP,)), D((NP,)), D((H, NP)), D((H, NP)),
         ],
         compiler_params=pltpu.CompilerParams(
-            collective_id=0, has_side_effects=True, vmem_limit_bytes=60 * 1024 * 1024),
-    )(queries, key_rows, values, in_gate.T, forget_gate.T, gain2)
+            collective_id=0, has_side_effects=True, vmem_limit_bytes=38 * 1024 * 1024),
+    )(*(pltpu.with_memory_space_constraint(x, pltpu.HBM) for x in (
+        queries, key_rows, values, in_gate.T, forget_gate.T, gain2)))
     return (jax.nn.sigmoid(out_gate.astype(F32)) * normed.astype(F32)).astype(BF16)
 
 

time: 61.7 us -> 60.7 us (0.984)
  other arithmetic: 5.96 us -> 3.67 us
  Pallas kernels: 55.5 us -> 56.8 us
    convert_element_type x1, other arithmetic: 5.96 us -> 3.67 us  [local(): (jax.nn.sigmoid(out_gate.astype(F32)) * normed.astype(F32)).astype(BF16)]
    pallas_call x1, Pallas kernels: 55.5 us -> 56.8 us  [local(): pl.pallas_call(functools.partial(kernel, n, m, H, NP), out_shape=jax.Shap...]
where the time goes in v3:
time: 60.7 us; the launch traced here: 60.5 us
  Pallas kernels  56.8 us (94%)
  other arithmetic  3.67 us (6%)
    pallas_call x1, Pallas kernels, local(): pl.pallas_call(functools.partial(kernel, n, m, H, NP), out_shape=jax.Shap...  56.8 us
    convert_element_type x1, other arithmetic, local(): (jax.nn.sigmoid(out_gate.astype(F32)) * normed.astype(F32)).astype(BF16)  3.67 us

profile of v3, /device:TPU:1, one launch (start us, length us, event | category | flops | bytes accessed | tf_op | source)
XLA Modules:
  0.0 60.5 jit_solution(10649361140442200781)
XLA Ops:
  0.0 0.0 copy-start
  0.0 56.8 %shard_map.73 = bf16[512,4096]{1,0:T(8,128)(2,1)S(1)} custom-call(bf16[512,2048]{1,0:T(8,128)(2,1)} %q_hbm.1, bf16[512,2048]{1,0:T(8,128)(2,1)} %k_hbm.1, bf16[512,4096]{1,0:T(8,128)(2,1)} %v_hbm.1, bf16[8,512]{1,0:T(8,128)(2,1)} %bitcast.3, bf16[8,512]{1,0:T(8,128)(2,1)} %bitcast.4, f32[1,2048]{1,0:T(1,128)} %bitcast.5), custom_call_target="tpu_custom_call" | custom-call | tf_op jit(solution)/shard_map/pallas_call | solution.py:310
  56.9 0.0 copy-done
  56.9 3.7 %multiply_convert_fusion = bf16[512,4096]{1,0:T(8,128)(2,1)} fusion(bf16[512,4096]{1,0:T(8,128)(2,1)S(1)} %shard_map.73, bf16[512,4096]{1,0:T(8,128)(2,1)S(1)} %copy-done), kind=kLoop, calls=%fused_computation | loop fusion | flops 14680064 | bytes 12582912 | tf_op jit(solution)/shard_map/convert_element_type | solution.py:331
Async XLA Ops:
  0.0 56.9 %copy-start = (bf16[512,4096]{1,0:T(8,128)(2,1)S(1)}, bf16[512,4096]{1,0:T(8,128)(2,1)}, u32[]{:S(2)}) copy-start(bf16[512,4096]{1,0:T(8,128)(2,1)} %param.12) | copy-start | bytes 12582916
